TPU v7x, 512 devices: a whole 4x4x16 slice. The times are simulated.
512 devices in a mesh: dp: 8 (over y, core), place: 64 (over x, z).
Axes of the slice: x: 4, y: 4, z: 16, core: 2. Of those that a mesh axis runs over, the one named last changes fastest.
Arguments:
- tokens: bfloat16 [8, 64, 256, 2048], P('dp', 'place'), may hold values from -6 to 6
- hidden_grad: bfloat16 [8, 64, 256, 256], P('dp', 'place'), may hold values from -6 to 6
- routing: int32 [8, 64, 4, 64], P('dp', 'place'), may hold values from 0 to 63, each once within a row
- row_count: int32 [8, 64], replicated, may hold values from 1 to 256, as said below
- old_slots: int32 [64], replicated, may hold values from 0 to 15, as said below
- new_slots: int32 [64], replicated, may hold values from 0 to 15, as said below
- master: float32 [16, 2048, 512], P(None, ('dp', 'place')), may hold values from -0.125 to 0.125
- first_moment: float32 [16, 2048, 512], P(None, ('dp', 'place')), may hold values from -0.018 to 0.018
- second_moment: float32 [16, 2048, 512], P(None, ('dp', 'place')), may hold values from 1e-06 to 0.0001
Outputs:
- new_weights: bfloat16 [64, 2048, 512], P('place')
- new_master: float32 [16, 2048, 512], P(None, ('dp', 'place'))
- new_first: float32 [16, 2048, 512], P(None, ('dp', 'place'))
- new_second: float32 [16, 2048, 512], P(None, ('dp', 'place'))
Inputs may be any that keep to these rules, and one draw needn't show every extreme that they name: `old_slots`: every expert 0 .. 15 holds at least one slot. `new_slots`: every expert 0 .. 15 holds at least one slot. The first row_count[d, p] of a device's 256 row slots are live; some device is full in every draw.
All inputs are finite; a program needn't handle non-finite values.
Results may differ from a plain program's by a relative error of at most 0.001.
The roundings to bfloat16 on the way count: a program that leaves them out, or rounds other values in their place, can miss the bound.
Values may be sent and summed in bfloat16 or wider, within the bound.
No kernel may reach another device: no remote copies, remote signals or barrier semaphores. Data moves between devices by JAX's collectives and lax.ppermute only.
A program may use at most 64 MiB of HBM per device.

v0:
```python
import jax
import jax.numpy as jnp
from jax import lax
from jax.sharding import PartitionSpec as P

decay_first = 0.9
decay_second = 0.95
learn_rate = 0.001
weight_decay = 0.1
epsilon = 1e-08
step_number = 20.0


def from_everyone(x, axis):
    copies = jnp.broadcast_to(x, (lax.axis_size(axis), *x.shape))
    return lax.all_to_all(copies, axis, split_axis=0, concat_axis=0, tiled=True)


def joined_along(parts, dim):
    lengths = list(parts.shape[1:])
    lengths[dim] *= parts.shape[0]
    return jnp.moveaxis(parts, 0, dim).reshape(lengths)


def gathered_copies(x, axis, dim):
    parts = from_everyone(x, axis)
    return joined_along(parts, dim)


def in_blocks(x, dim, peers):
    before, after = (x.shape[:dim], x.shape[dim + 1 :])
    return jnp.moveaxis(x.reshape(*before, peers, -1, *after), dim, 0)


def sent_and_summed(x, axis, dim):
    peers = lax.axis_size(axis)
    parts = lax.all_to_all(in_blocks(x, dim, peers), axis, 0, 0, tiled=True)
    return jnp.sum(parts, axis=0)


def spread(shard, slots):
    experts, rows_shard, width = shard.shape
    places = lax.axis_size("place")
    select = (slots[:, None] == jnp.arange(experts, dtype=jnp.int32)[None, :]).astype(jnp.bfloat16)
    picked = jnp.dot(
        select, shard.reshape(experts, rows_shard * width), preferred_element_type=jnp.float32
    ).astype(jnp.bfloat16)
    landed = lax.all_to_all(
        picked.reshape(places, rows_shard, width), "place", split_axis=0, concat_axis=0, tiled=True
    )
    whole = gathered_copies(landed.reshape(places * rows_shard, width), "dp", 0)
    return whole


def batch_grad(total, rows_in, grads_in, order, count, weights, start):
    rows = order.shape[0]
    half = weights.shape[1] // 2
    picked = jnp.take(rows_in, start + order, axis=0)
    both = jnp.dot(picked, weights, preferred_element_type=jnp.float32)
    gate = both[:, :half]
    upward = both[:, half:]
    sigma = jax.nn.sigmoid(gate)
    active = gate * sigma
    slope = sigma * (1.0 + gate * (1.0 - sigma))
    live = start + jnp.arange(rows, dtype=jnp.int32) < count
    incoming = jnp.where(live[:, None], grads_in[start : start + rows].astype(jnp.float32), 0.0)
    local = jnp.concatenate([incoming * upward * slope, incoming * active], axis=1).astype(
        jnp.bfloat16
    )
    return total + lax.dot_general(
        picked, local, (((0,), (0,)), ((), ())), preferred_element_type=jnp.float32
    )


def shards(
    tokens,
    hidden_grad,
    routing,
    row_count,
    old_slots,
    new_slots,
    master,
    first_moment,
    second_moment,
):
    places = lax.axis_size("place")
    groups = lax.axis_size("dp")
    experts, rows_shard, width = master.shape
    place_here = lax.axis_index("place")
    group_here = lax.axis_index("dp")
    weights = spread(master.astype(jnp.bfloat16), old_slots)
    rows_in = tokens[0, 0]
    grads_in = hidden_grad[0, 0]
    order = routing[0, 0]
    count = row_count[group_here, place_here]
    batch_rows = order.shape[1]
    summed = jnp.zeros((rows_in.shape[1], width), jnp.float32)
    for batch_index in range(order.shape[0]):
        start = batch_index * batch_rows
        summed = batch_grad(summed, rows_in, grads_in, order[batch_index], count, weights, start)
    select = (old_slots[:, None] == jnp.arange(experts, dtype=jnp.int32)[None, :]).astype(
        jnp.float32
    )
    blocks = summed.reshape(groups, places, rows_shard, width)
    partial_sum = sent_and_summed(blocks, "dp", 0)
    landed = lax.all_to_all(partial_sum, "place", split_axis=1, concat_axis=1, tiled=True)
    grad_sum = jnp.dot(
        select.T, landed.reshape(places, rows_shard * width), precision=lax.Precision.HIGHEST
    ).reshape(experts, rows_shard, width)
    per_slot = jnp.sum(row_count.astype(jnp.float32), axis=0)
    total = jnp.dot(per_slot, select, precision=lax.Precision.HIGHEST)
    grad = grad_sum / total[:, None, None]
    new_first = decay_first * first_moment + (1.0 - decay_first) * grad
    new_second = decay_second * second_moment + (1.0 - decay_second) * grad * grad
    first_hat = new_first / (1.0 - decay_first**step_number)
    second_hat = new_second / (1.0 - decay_second**step_number)
    new_master = master - learn_rate * (
        first_hat / (jnp.sqrt(second_hat) + epsilon) + weight_decay * master
    )
    new_weights = spread(new_master.astype(jnp.bfloat16), new_slots)
    return (new_weights[None], new_master, new_first, new_second)


def solution(mesh):
    placed = (
        P("dp", "place", None, None),
        P("dp", "place", None, None),
        P("dp", "place", None, None),
        P(),
        P(),
        P(),
        P(None, ("dp", "place"), None),
        P(None, ("dp", "place"), None),
        P(None, ("dp", "place"), None),
    )
    return jax.shard_map(
        shards,
        mesh=mesh,
        in_specs=placed,
        out_specs=(
            P("place", None, None),
            P(None, ("dp", "place"), None),
            P(None, ("dp", "place"), None),
            P(None, ("dp", "place"), None),
        ),
        check_vma=False,
    )
```

profile of v0, /device:TPU:1, one launch (start us, length us, event | category | flops | bytes accessed | tf_op | source)
XLA Modules:
  0.0 247.8 jit_solution(2621490347751096984)
XLA Ops:
  0.6 1.0 convert_element_type.48
  1.7 0.9 convolution_convert_fusion.1
  2.8 38.0 %all_to_all.30 = bf16[64,4,512]{2,1,0:T(4,128)(2,1)S(1)} all-to-all(bf16[64,4,512]{2,1,0:T(4,128)(2,1)S(1)} %reshape.89), channel_id=1, replica_groups=mesh['dp'=8,'place'=64] {'place'}, dimensions={0} | all-to-all | bytes 524288 | tf_op jit(solution)/shard_map/all_to_all | solution.py:48
  40.9 1.5 broadcast_in_dim.58
  42.4 7.5 %all-to-all-start.1 = ((bf16[8,256,512]{2,1,0:T(8,128)(2,1)}), bf16[8,256,512]{2,1,0:T(8,128)(2,1)S(1)}, u32[]{:S(2)}, u32[]{:S(2)}) async-start(bf16[8,256,512]{2,1,0:T(8,128)(2,1)} %broadcast_in_dim.58), calls=%async_computation.1 | async-start | bytes 4194304 | tf_op jit(solution)/shard_map/all_to_all | solution.py:16
  49.9 1.4 gather_fusion
  51.3 1.4 gather_fusion.1
  53.5 1.4 gather_fusion.2
  56.9 19.2 %all-to-all-done.1 = bf16[8,256,512]{2,1,0:T(8,128)(2,1)S(1)} async-done(((bf16[8,256,512]{2,1,0:T(8,128)(2,1)}), bf16[8,256,512]{2,1,0:T(8,128)(2,1)S(1)}, u32[]{:S(2)}, u32[]{:S(2)}) %all-to-all-start.1) | async-done | bytes 2097184 | tf_op jit(solution)/shard_map/all_to_all | solution.py:16
  76.0 1.5 fusion.5
  78.8 0.8 fusion.6
  79.7 0.8 fusion.4
  81.3 0.8 fusion.8
  82.1 2.8 %add_add_fusion = f32[2048,512]{1,0:T(8,128)} fusion(f32[2048,512]{1,0:T(8,128)S(1)} %fusion.8, f32[2048,512]{1,0:T(8,128)S(1)} %fusion.4, f32[2048,512]{1,0:T(8,128)S(1)} %fusion.6, bf16[64,2048]{1,0:T(8,128)(2,1)S(1)} %gather_fusion.3, pred[64]{0:T(512)(128)(4,1)S(1)} %get-tuple-element.21, bf16[64,256]{1,0:T(8,128)(2,1)S(1)} %get-tuple-element.30, ...), kind=kOutput, calls=%fused_computation.4 | convolution fusion | flops 137625600 | bytes 17104960 | tf_op jit(solution)/shard_map/dot_general | solution.py:70
  84.9 5.2 %reshape_reshape.3 = f32[8,1,64,4,512]{4,3,2,0,1:T(4,128)} reshape(f32[2048,512]{1,0:T(8,128)} %add_add_fusion) | data formatting | bytes 8388608 | tf_op jit(solution)/shard_map/reshape;reshape | solution.py:32
  90.1 54.1 %all_to_all.31 = f32[8,1,64,4,512]{4,3,2,1,0:T(4,128)} all-to-all(f32[8,1,64,4,512]{4,3,2,1,0:T(4,128)} %bitcast.78), channel_id=1, replica_groups=mesh['dp'=8,'place'=64] {'dp'}, dimensions={0} | all-to-all | bytes 8388608 | tf_op jit(solution)/shard_map/all_to_all | solution.py:37
  144.2 3.9 %reduce_sum.20 = f32[64,4,512]{2,1,0:T(4,128)} reduce(f32[8,1,64,4,512]{4,3,2,1,0:T(4,128)} %all_to_all.31, f32[]{:T(128)} %constant.16.clone.1), dimensions={0,1}, to_apply=%region_0.0 | reduce | flops 917504 | bytes 4718596 | tf_op jit(solution)/shard_map/reduce_sum | solution.py:38
  148.1 6.3 %all-to-all-start.3 = ((f32[1,64,4,512]{3,2,0,1:T(4,128)}), f32[1,64,4,512]{3,2,0,1:T(4,128)S(1)}, u32[]{:S(2)}, u32[]{:S(2)}) async-start(f32[1,64,4,512]{3,2,0,1:T(4,128)} %bitcast.13), calls=%async_computation.3 | async-start | bytes 1048576 | tf_op jit(solution)/shard_map/all_to_all | solution.py:106
  154.5 29.2 %all-to-all-done.3 = f32[1,64,4,512]{3,2,0,1:T(4,128)S(1)} async-done(((f32[1,64,4,512]{3,2,0,1:T(4,128)}), f32[1,64,4,512]{3,2,0,1:T(4,128)S(1)}, u32[]{:S(2)}, u32[]{:S(2)}) %all-to-all-start.3) | async-done | bytes 524320 | tf_op jit(solution)/shard_map/all_to_all | solution.py:106
  184.8 27.1 %all_to_all.32 = bf16[64,4,512]{2,1,0:T(4,128)(2,1)S(1)} all-to-all(bf16[64,4,512]{2,1,0:T(4,128)(2,1)S(1)} %reshape.94), channel_id=1, replica_groups=mesh['dp'=8,'place'=64] {'place'}, dimensions={0} | all-to-all | bytes 524288 | tf_op jit(solution)/shard_map/all_to_all | solution.py:48
  212.0 1.5 broadcast_in_dim.62
  213.5 6.7 %all-to-all-start.5 = ((bf16[8,256,512]{2,1,0:T(8,128)(2,1)}), bf16[8,256,512]{2,1,0:T(8,128)(2,1)S(1)}, u32[]{:S(2)}, u32[]{:S(2)}) async-start(bf16[8,256,512]{2,1,0:T(8,128)(2,1)} %broadcast_in_dim.62), calls=%async_computation.5 | async-start | bytes 4194304 | tf_op jit(solution)/shard_map/all_to_all | solution.py:16
  222.5 24.0 %all-to-all-done.5 = bf16[8,256,512]{2,1,0:T(8,128)(2,1)S(1)} async-done(((bf16[8,256,512]{2,1,0:T(8,128)(2,1)}), bf16[8,256,512]{2,1,0:T(8,128)(2,1)S(1)}, u32[]{:S(2)}, u32[]{:S(2)}) %all-to-all-start.5) | async-done | bytes 2097184 | tf_op jit(solution)/shard_map/all_to_all | solution.py:16
  246.5 1.3 copy.63
  (49 shorter events, 8.4 us)
Async XLA Ops:
  0.6 49.2 %copy-start = (bf16[1,1,256,2048]{3,2,1,0:T(8,128)(2,1)S(1)}, bf16[1,1,256,2048]{3,2,1,0:T(8,128)(2,1)}, u32[]{:S(2)}) copy-start(bf16[1,1,256,2048]{3,2,1,0:T(8,128)(2,1)} %param.11) | copy-start | bytes 3145732
  42.4 7.5 %copy-start.7 = (s32[1,1,4,64]{3,2,1,0:T(4,128)S(1)}, s32[1,1,4,64]{3,2,1,0:T(4,128)}, u32[]{:S(2)}) copy-start(s32[1,1,4,64]{3,2,1,0:T(4,128)} %param.13) | copy-start | bytes 3076
  42.4 33.7 %all-to-all-start.1 = ((bf16[8,256,512]{2,1,0:T(8,128)(2,1)}), bf16[8,256,512]{2,1,0:T(8,128)(2,1)S(1)}, u32[]{:S(2)}, u32[]{:S(2)}) async-start(bf16[8,256,512]{2,1,0:T(8,128)(2,1)} %broadcast_in_dim.58), calls=%async_computation.1 | async-start | bytes 4194304 | tf_op jit(solution)/shard_map/all_to_all | solution.py:16
  52.8 2.2 copy-start.6
  76.0 1.5 copy-start.2
  77.6 1.1 copy-start.4
  78.8 1.0 copy-start.1
  79.7 0.9 copy-start.3
  144.2 10.2 %copy-start.8 = (s32[64]{0:T(128)S(1)}, s32[64]{0:T(128)}, u32[]{:S(2)}) copy-start(s32[64]{0:T(128)} %param.15) | copy-start | bytes 772
  144.2 39.5 %copy-start.5 = (f32[16,4,512]{2,1,0:T(4,128)S(1)}, f32[16,4,512]{2,1,0:T(4,128)}, u32[]{:S(2)}) copy-start(f32[16,4,512]{2,1,0:T(4,128)} %param.17) | copy-start | bytes 393220
  144.2 39.5 %copy-start.10 = (f32[16,4,512]{2,1,0:T(4,128)S(1)}, f32[16,4,512]{2,1,0:T(4,128)}, u32[]{:S(2)}) copy-start(f32[16,4,512]{2,1,0:T(4,128)} %param.18) | copy-start | bytes 393220
  144.2 39.5 %copy-start.11 = (f32[16,4,512]{2,1,0:T(4,128)S(1)}, f32[16,4,512]{2,1,0:T(4,128)}, u32[]{:S(2)}) copy-start(f32[16,4,512]{2,1,0:T(4,128)} %param.19) | copy-start | bytes 393220
  148.1 36.2 %copy-start.9 = (s32[64]{0:T(128)S(1)}, s32[64]{0:T(128)}, u32[]{:S(2)}) copy-start(s32[64]{0:T(128)} %param.16) | copy-start | bytes 772
  148.1 35.6 %all-to-all-start.3 = ((f32[1,64,4,512]{3,2,0,1:T(4,128)}), f32[1,64,4,512]{3,2,0,1:T(4,128)S(1)}, u32[]{:S(2)}, u32[]{:S(2)}) async-start(f32[1,64,4,512]{3,2,0,1:T(4,128)} %bitcast.13), calls=%async_computation.3 | async-start | bytes 1048576 | tf_op jit(solution)/shard_map/all_to_all | solution.py:106
  213.5 33.0 %all-to-all-start.5 = ((bf16[8,256,512]{2,1,0:T(8,128)(2,1)}), bf16[8,256,512]{2,1,0:T(8,128)(2,1)S(1)}, u32[]{:S(2)}, u32[]{:S(2)}) async-start(bf16[8,256,512]{2,1,0:T(8,128)(2,1)} %broadcast_in_dim.62), calls=%async_computation.5 | async-start | bytes 4194304 | tf_op jit(solution)/shard_map/all_to_all | solution.py:16
where the time goes:
time: 248 us
  blocking collectives  119 us (48%)
  waiting for transfers between devices  72.4 us (29%)
  starting transfers between devices  20.5 us (8%)
  local copies, waits for them, and re-layouts  18.2 us (7%)
  matrix products  10.2 us (4%)
  other arithmetic  6.47 us (3%)
    all_to_all x2, blocking collectives, spread(): lax.all_to_all(picked.reshape(places, rows_shard, width), 'place', split_...  65.1 us
    all_to_all x1, blocking collectives, sent_and_summed(): parts = lax.all_to_all(in_blocks(x, dim, peers), axis, 0, 0, tiled=True)  54.1 us
    all_to_all x2, waiting for transfers between devices, from_everyone(): return lax.all_to_all(copies, axis, split_axis=0, concat_axis=0, tiled=True)  43.2 us
    all_to_all x1, waiting for transfers between devices, shards(): lax.all_to_all(partial_sum, 'place', split_axis=1, concat_axis=1, tiled=T...  29.2 us
    all_to_all x2, starting transfers between devices, from_everyone(): return lax.all_to_all(copies, axis, split_axis=0, concat_axis=0, tiled=True)  14.2 us
    all_to_all x1, starting transfers between devices, shards(): lax.all_to_all(partial_sum, 'place', split_axis=1, concat_axis=1, tiled=T...  6.27 us
    dot_general x4, matrix products, batch_grad(): lax.dot_general(picked, local, (((0,), (0,)), ((), ())), preferred_elemen...  5.23 us
    another operation x1, local copies, waits for them, and re-layouts, in_blocks(): return jnp.moveaxis(x.reshape(*before, peers, -1, *after), dim, 0)  5.18 us
  transfers between devices with their start and end apart: 3, of which 3 were waited for; matrix products, arithmetic and copies ran while one was open for 4% of the time, Pallas kernels for 0%

commit v1 on v0

--- a/solution.py
+++ b/solution.py
@@ -9,6 +9,13 @@
 weight_decay = 0.1
 epsilon = 1e-08
 step_number = 20.0
+
+
+def cube_end(target):
+    m_next = lax.axis_size("place")
+    r2 = jnp.stack(jnp.split(target, m_next, axis=1))
+    tall = lax.all_to_all(r2, "place", 0, 0)
+    return jnp.concatenate(tall, axis=1)
 
 
 def from_everyone(x, axis):
@@ -103,7 +110,7 @@
     )
     blocks = summed.reshape(groups, places, rows_shard, width)
     partial_sum = sent_and_summed(blocks, "dp", 0)
-    landed = lax.all_to_all(partial_sum, "place", split_axis=1, concat_axis=1, tiled=True)
+    landed = cube_end(partial_sum)
     grad_sum = jnp.dot(
         select.T, landed.reshape(places, rows_shard * width), precision=lax.Precision.HIGHEST
     ).reshape(experts, rows_shard, width)

time: 248 us -> 286 us (1.15)
  local copies, waits for them, and re-layouts: 18.2 us -> 56.6 us
    unnamed x29 -> x92, local copies, waits for them, and re-layouts: 3.87 us -> 41.6 us
  transfers between devices with their start and end apart: 3 -> 3, of which waited for: 3 -> 3; matrix products, arithmetic and copies ran while one was open for 4% -> 3% of each run, Pallas kernels for 0% -> 0%
where the time goes in v1:
time: 286 us; the launch traced here: 285 us
  blocking collectives  119 us (42%)
  waiting for transfers between devices  72.4 us (25%)
  local copies, waits for them, and re-layouts  56.6 us (20%)
  starting transfers between devices  20.3 us (7%)
  matrix products  10.2 us (4%)
  other arithmetic  5.56 us (2%)
    all_to_all x2, blocking collectives, spread(): lax.all_to_all(picked.reshape(places, rows_shard, width), 'place', split_...  65.1 us
    all_to_all x1, blocking collectives, sent_and_summed(): parts = lax.all_to_all(in_blocks(x, dim, peers), axis, 0, 0, tiled=True)  54.1 us
    all_to_all x2, waiting for transfers between devices, from_everyone(): return lax.all_to_all(copies, axis, split_axis=0, concat_axis=0, tiled=True)  43.2 us
    unnamed x92, local copies, waits for them, and re-layouts  41.6 us
    all_to_all x1, waiting for transfers between devices, cube_end(): tall = lax.all_to_all(r2, 'place', 0, 0)  29.2 us
    all_to_all x2, starting transfers between devices, from_everyone(): return lax.all_to_all(copies, axis, split_axis=0, concat_axis=0, tiled=True)  14.2 us
    all_to_all x1, starting transfers between devices, cube_end(): tall = lax.all_to_all(r2, 'place', 0, 0)  6.14 us
  transfers between devices with their start and end apart: 3, of which 3 were waited for; matrix products, arithmetic and copies ran while one was open for 3% of the time, Pallas kernels for 0%

profile of v1, /device:TPU:1, one launch (start us, length us, event | category | flops | bytes accessed | tf_op | source)
XLA Modules:
  0.0 285.2 jit_solution(11843191302656856019)
XLA Ops:
  0.6 1.0 convert_element_type.48
  1.7 0.9 convolution_convert_fusion.1
  2.8 38.0 %all_to_all.30 = bf16[64,4,512]{2,1,0:T(4,128)(2,1)S(1)} all-to-all(bf16[64,4,512]{2,1,0:T(4,128)(2,1)S(1)} %reshape.86), channel_id=1, replica_groups=mesh['dp'=8,'place'=64] {'place'}, dimensions={0} | all-to-all | bytes 524288 | tf_op jit(solution)/shard_map/all_to_all | solution.py:55
  40.9 1.5 broadcast_in_dim.58
  42.4 7.5 %all-to-all-start.1 = ((bf16[8,256,512]{2,1,0:T(8,128)(2,1)}), bf16[8,256,512]{2,1,0:T(8,128)(2,1)S(1)}, u32[]{:S(2)}, u32[]{:S(2)}) async-start(bf16[8,256,512]{2,1,0:T(8,128)(2,1)} %broadcast_in_dim.58), calls=%async_computation.1 | async-start | bytes 4194304 | tf_op jit(solution)/shard_map/all_to_all | solution.py:23
  49.9 1.4 gather_fusion
  51.3 1.4 gather_fusion.1
  53.5 1.4 gather_fusion.2
  56.9 19.2 %all-to-all-done.1 = bf16[8,256,512]{2,1,0:T(8,128)(2,1)S(1)} async-done(((bf16[8,256,512]{2,1,0:T(8,128)(2,1)}), bf16[8,256,512]{2,1,0:T(8,128)(2,1)S(1)}, u32[]{:S(2)}, u32[]{:S(2)}) %all-to-all-start.1) | async-done | bytes 2097184 | tf_op jit(solution)/shard_map/all_to_all | solution.py:23
  76.0 1.5 fusion.5
  78.8 0.8 fusion.6
  79.7 0.8 fusion.4
  81.3 0.8 fusion.8
  82.1 2.8 add_add_fusion
  84.9 5.2 %reshape_reshape.6 = f32[8,1,64,4,512]{4,3,2,0,1:T(4,128)} reshape(f32[2048,512]{1,0:T(8,128)} %add_add_fusion) | data formatting | bytes 8388608 | tf_op jit(solution)/shard_map/reshape;reshape | solution.py:39
  90.1 54.1 %all_to_all.31 = f32[8,1,64,4,512]{4,3,2,1,0:T(4,128)} all-to-all(f32[8,1,64,4,512]{4,3,2,1,0:T(4,128)} %bitcast.333), channel_id=1, replica_groups=mesh['dp'=8,'place'=64] {'dp'}, dimensions={0} | all-to-all | bytes 8388608 | tf_op jit(solution)/shard_map/all_to_all | solution.py:44
  144.2 3.0 %reduce_sum.20 = f32[64,4,512]{2,1,0:T(4,128)S(1)} reduce(f32[8,1,64,4,512]{4,3,2,1,0:T(4,128)} %all_to_all.31, f32[]{:T(128)} %constant.16.clone.1), dimensions={0,1}, to_apply=%region_0.0 | reduce | flops 917504 | bytes 4718596 | tf_op jit(solution)/shard_map/reduce_sum | solution.py:45
  185.6 6.1 %all-to-all-start.3 = ((f32[64,1,1,4,512]{4,3,2,1,0:T(4,128)}), f32[64,1,1,4,512]{4,3,2,1,0:T(4,128)S(1)}, u32[]{:S(2)}, u32[]{:S(2)}) async-start(f32[64,1,1,4,512]{4,3,2,1,0:T(4,128)} %constant_dynamic-update-slice_fusion), calls=%async_computation.3 | async-start | bytes 1048576 | tf_op jit(solution)/shard_map/all_to_all | solution.py:17
  191.9 29.2 %all-to-all-done.3 = f32[64,1,1,4,512]{4,3,2,1,0:T(4,128)S(1)} async-done(((f32[64,1,1,4,512]{4,3,2,1,0:T(4,128)}), f32[64,1,1,4,512]{4,3,2,1,0:T(4,128)S(1)}, u32[]{:S(2)}, u32[]{:S(2)}) %all-to-all-start.3) | async-done | bytes 524320 | tf_op jit(solution)/shard_map/all_to_all | solution.py:17
  222.1 27.1 %all_to_all.32 = bf16[64,4,512]{2,1,0:T(4,128)(2,1)S(1)} all-to-all(bf16[64,4,512]{2,1,0:T(4,128)(2,1)S(1)} %reshape.90), channel_id=1, replica_groups=mesh['dp'=8,'place'=64] {'place'}, dimensions={0} | all-to-all | bytes 524288 | tf_op jit(solution)/shard_map/all_to_all | solution.py:55
  249.4 1.5 broadcast_in_dim.62
  250.9 6.7 %all-to-all-start.5 = ((bf16[8,256,512]{2,1,0:T(8,128)(2,1)}), bf16[8,256,512]{2,1,0:T(8,128)(2,1)S(1)}, u32[]{:S(2)}, u32[]{:S(2)}) async-start(bf16[8,256,512]{2,1,0:T(8,128)(2,1)} %broadcast_in_dim.62), calls=%async_computation.5 | async-start | bytes 4194304 | tf_op jit(solution)/shard_map/all_to_all | solution.py:23
  259.8 24.0 %all-to-all-done.5 = bf16[8,256,512]{2,1,0:T(8,128)(2,1)S(1)} async-done(((bf16[8,256,512]{2,1,0:T(8,128)(2,1)}), bf16[8,256,512]{2,1,0:T(8,128)(2,1)S(1)}, u32[]{:S(2)}, u32[]{:S(2)}) %all-to-all-start.5) | async-done | bytes 2097184 | tf_op jit(solution)/shard_map/all_to_all | solution.py:23
  283.8 1.3 copy.189
  (113 shorter events, 46.8 us)
Async XLA Ops:
  0.6 49.2 %copy-start = (bf16[1,1,256,2048]{3,2,1,0:T(8,128)(2,1)S(1)}, bf16[1,1,256,2048]{3,2,1,0:T(8,128)(2,1)}, u32[]{:S(2)}) copy-start(bf16[1,1,256,2048]{3,2,1,0:T(8,128)(2,1)} %param.11) | copy-start | bytes 3145732
  42.4 7.5 %copy-start.7 = (s32[1,1,4,64]{3,2,1,0:T(4,128)S(1)}, s32[1,1,4,64]{3,2,1,0:T(4,128)}, u32[]{:S(2)}) copy-start(s32[1,1,4,64]{3,2,1,0:T(4,128)} %param.13) | copy-start | bytes 3076
  42.4 33.7 %all-to-all-start.1 = ((bf16[8,256,512]{2,1,0:T(8,128)(2,1)}), bf16[8,256,512]{2,1,0:T(8,128)(2,1)S(1)}, u32[]{:S(2)}, u32[]{:S(2)}) async-start(bf16[8,256,512]{2,1,0:T(8,128)(2,1)} %broadcast_in_dim.58), calls=%async_computation.1 | async-start | bytes 4194304 | tf_op jit(solution)/shard_map/all_to_all | solution.py:23
  52.8 2.2 copy-start.6
  76.0 1.5 copy-start.2
  77.6 1.1 copy-start.4
  78.8 1.0 copy-start.1
  79.7 0.9 copy-start.3
  147.2 44.6 %copy-start.8 = (s32[64]{0:T(128)S(1)}, s32[64]{0:T(128)}, u32[]{:S(2)}) copy-start(s32[64]{0:T(128)} %param.15) | copy-start | bytes 772
  147.2 73.9 %copy-start.5 = (f32[16,4,512]{2,1,0:T(4,128)S(1)}, f32[16,4,512]{2,1,0:T(4,128)}, u32[]{:S(2)}) copy-start(f32[16,4,512]{2,1,0:T(4,128)} %param.17) | copy-start | bytes 393220
  147.2 73.9 %copy-start.10 = (f32[16,4,512]{2,1,0:T(4,128)S(1)}, f32[16,4,512]{2,1,0:T(4,128)}, u32[]{:S(2)}) copy-start(f32[16,4,512]{2,1,0:T(4,128)} %param.18) | copy-start | bytes 393220
  147.2 73.9 %copy-start.11 = (f32[16,4,512]{2,1,0:T(4,128)S(1)}, f32[16,4,512]{2,1,0:T(4,128)}, u32[]{:S(2)}) copy-start(f32[16,4,512]{2,1,0:T(4,128)} %param.19) | copy-start | bytes 393220
  147.2 74.5 %copy-start.9 = (s32[64]{0:T(128)S(1)}, s32[64]{0:T(128)}, u32[]{:S(2)}) copy-start(s32[64]{0:T(128)} %param.16) | copy-start | bytes 772
  185.6 35.5 %all-to-all-start.3 = ((f32[64,1,1,4,512]{4,3,2,1,0:T(4,128)}), f32[64,1,1,4,512]{4,3,2,1,0:T(4,128)S(1)}, u32[]{:S(2)}, u32[]{:S(2)}) async-start(f32[64,1,1,4,512]{4,3,2,1,0:T(4,128)} %constant_dynamic-update-slice_fusion), calls=%async_computation.3 | async-start | bytes 1048576 | tf_op jit(solution)/shard_map/all_to_all | solution.py:17
  250.9 33.0 %all-to-all-start.5 = ((bf16[8,256,512]{2,1,0:T(8,128)(2,1)}), bf16[8,256,512]{2,1,0:T(8,128)(2,1)S(1)}, u32[]{:S(2)}, u32[]{:S(2)}) async-start(bf16[8,256,512]{2,1,0:T(8,128)(2,1)} %broadcast_in_dim.62), calls=%async_computation.5 | async-start | bytes 4194304 | tf_op jit(solution)/shard_map/all_to_all | solution.py:23
